TPU v7x, 128 devices: a whole 4x4x4 slice. The times are simulated.
128 devices in a mesh: shot: 32 (over z, y, core), tm: 4 (over x).
Axes of the slice: x: 4, y: 4, z: 4, core: 2. Of those that a mesh axis runs over, the one named last changes fastest.
Arguments:
- signals: bfloat16 [256, 128, 2048], P('tm', 'shot'), may hold values from -0.59765625 to 0.59765625
- aperture: int32 [128, 128, 128], P('shot'), may hold values from 0 to 2047
- counts: int32 [128, 128], P('shot'), may hold values from 97 to 128, as said below
Outputs:
- prediction: float32 [256, 128, 128], P('tm', None, 'shot')
Inputs may be any that keep to these rules, and one draw needn't show every extreme that they name: Slots j >= counts[r, s] of aperture[r, s] are padding and do not enter the prediction. `counts`: in every draw some output trace uses all 128 slots.
All inputs are finite; a program needn't handle non-finite values.
Results may differ from a plain program's by a relative error of at most 0.0003.
Values may be sent and summed in bfloat16 or wider, within the bound.
No kernel may reach another device: no remote copies, remote signals or barrier semaphores. Data moves between devices by JAX's collectives and lax.ppermute only.
A program may use at most 128 MiB of HBM per device.

v0:
```python
import math
import jax
import jax.numpy as jnp
from jax import lax
from jax.sharding import PartitionSpec as P


def spectra_tables(length):
    sample_ids = jnp.arange(length, dtype=jnp.int32)
    freq_ids = jnp.concatenate(
        [jnp.arange(length + 1, dtype=jnp.int32), jnp.arange(1, length, dtype=jnp.int32)]
    )
    phases = sample_ids[:, None] * freq_ids[None, :] % (2 * length)
    angles = phases.astype(jnp.float32) * (math.pi / length)
    columns = jnp.arange(2 * length, dtype=jnp.int32)
    forward = jnp.where(columns[None, :] <= length, jnp.cos(angles), -jnp.sin(angles))
    weights = jnp.where((freq_ids == 0) | (freq_ids == length), 1.0, 2.0) / (2.0 * length)
    inverse = (
        jnp.where(columns[:, None] <= length, jnp.cos(angles.T), -jnp.sin(angles.T))
        * weights[:, None]
    )
    return (forward, inverse)


def spectral_product(spec_a, spec_b, length):
    real_a = spec_a[..., : length + 1]
    imag_a = spec_a[..., length + 1 :]
    real_b = spec_b[..., : length + 1]
    imag_b = spec_b[..., length + 1 :]
    real_part = real_a * real_b
    middle = real_part[..., 1:length] - imag_a * imag_b
    real_part = jnp.concatenate([real_part[..., :1], middle, real_part[..., length:]], axis=-1)
    imag_part = real_a[..., 1:length] * imag_b + imag_a * real_b[..., 1:length]
    return jnp.concatenate([real_part, imag_part], axis=-1)


def predict(first_side, second_side):
    length, count_s, count_r, span_len = first_side.shape
    forward, inverse = spectra_tables(length)
    block_len = count_s
    for candidate in range(count_s, 0, -1):
        if count_s % candidate == 0 and candidate * count_r * span_len >= 512:
            block_len = candidate
    blocks = count_s // block_len

    def one_block(block_idx):
        part_a = lax.dynamic_slice_in_dim(first_side, block_idx * block_len, block_len, 1).astype(
            jnp.float32
        )
        part_b = lax.dynamic_slice_in_dim(second_side, block_idx * block_len, block_len, 1).astype(
            jnp.float32
        )
        spec_a = jnp.einsum("tsrj,tk->srjk", part_a, forward, precision=lax.Precision.HIGHEST)
        spec_b = jnp.einsum("tsrj,tk->srjk", part_b, forward, precision=lax.Precision.HIGHEST)
        return jnp.sum(spectral_product(spec_a, spec_b, length), axis=2)

    spectra = lax.map(one_block, jnp.arange(blocks, dtype=jnp.int32))
    spectra = spectra.reshape(count_s, count_r, 2 * length)
    return jnp.einsum("srk,kt->tsr", spectra, inverse, precision=lax.Precision.HIGHEST)


def convolve(halves):
    return predict(halves[0], halves[1])


def body(signals, aperture, counts):
    length_win, shots_here, stations = signals.shape
    span_len = aperture.shape[2]
    offsets = jnp.arange(shots_here, dtype=jnp.int32) * stations
    gathered_lists = lax.all_to_all(aperture, "shot", split_axis=1, concat_axis=0, tiled=True)
    live_mask = jnp.arange(span_len, dtype=jnp.int32)[None, None, :] < counts[:, :, None]
    live_mask = jnp.transpose(live_mask, (1, 0, 2))
    own_index = jnp.transpose(aperture + offsets[:, None, None], (1, 0, 2))
    sender_index = jnp.transpose(gathered_lists + offsets[None, :, None], (1, 0, 2))
    flat_signals = signals.reshape(length_win, shots_here * stations)
    own_traces = jnp.take(flat_signals, own_index, axis=1)
    local_side = jnp.where(live_mask[None], own_traces, jnp.zeros_like(own_traces))
    remote_side = jnp.take(flat_signals, sender_index, axis=1)
    arrived = lax.all_to_all(remote_side, "shot", split_axis=2, concat_axis=1, tiled=True)
    merged = convolve(
        (
            lax.all_to_all(arrived, "tm", split_axis=1, concat_axis=0, tiled=True),
            lax.all_to_all(local_side, "tm", split_axis=1, concat_axis=0, tiled=True),
        )
    )
    result = lax.all_to_all(merged, "tm", split_axis=0, concat_axis=1, tiled=True)
    return result


def solution(mesh):
    in_specs = (P("tm", "shot", None), P("shot", None, None), P("shot", None))
    out_specs = P("tm", None, "shot")
    return jax.shard_map(body, mesh=mesh, in_specs=in_specs, out_specs=out_specs, check_vma=False)
```

profile of v0, /device:TPU:8, one launch (start us, length us, event | category | flops | bytes accessed | tf_op | source)
XLA Modules:
  0.0 1156.7 jit_solution(7991697897503498598)
XLA Ops:
  1.8 8.5 all-to-all-start
  13.3 4.8 all-to-all-done
  18.3 229.0 %gather_fusion = bf16[65536,64]{1,0:T(8,128)(2,1)} fusion(bf16[64,8192]{0,1:T(8,128)(2,1)S(1)} %bitcast.76, s32[65536]{0:T(1024)S(1)} %broadcast_clamp_fusion.1), kind=kCustom, calls=%fused_computation | custom fusion | bytes 17039360 | tf_op jit(solution)/shard_map/jit(_take)/gather | solution.py:78
  247.3 15.8 %copy.40 = bf16[4,128,128,64]{2,3,0,1:T(8,128)(2,1)} copy(bf16[4,128,128,64]{3,2,1,0:T(8,128)(2,1)} %bitcast.79) | data formatting | bytes 16777216 | tf_op jit(solution)/shard_map/jit(_take)/gather | solution.py:78
  263.3 7.6 select_bitcast_fusion.1
  270.8 6.1 all-to-all-start.1
  277.4 229.0 %gather_fusion.1 = bf16[65536,64]{1,0:T(8,128)(2,1)} fusion(bf16[64,8192]{0,1:T(8,128)(2,1)S(1)} %bitcast.77, s32[65536]{0:T(1024)S(1)} %broadcast_clamp_fusion), kind=kCustom, calls=%fused_computation.1 | custom fusion | bytes 17039360 | tf_op jit(solution)/shard_map/jit(_take)/gather | solution.py:76
  506.4 19.1 %copy.48 = bf16[128,4,128,64]{2,1,3,0:T(4,128)(2,1)} copy(bf16[128,4,128,64]{3,2,1,0:T(8,128)(2,1)} %bitcast.78) | data formatting | bytes 16777216 | tf_op jit(solution)/shard_map/jit(_take)/gather | solution.py:76
  525.9 8.5 select_bitcast_fusion
  534.4 5.6 all-to-all-start.3
  540.0 9.6 copy.42
  549.7 84.8 %all-to-all-done.3 = bf16[64,128,4,128]{3,2,0,1:T(4,128)(2,1)} async-done(((bf16[64,128,4,128]{3,2,0,1:T(4,128)(2,1)}), bf16[64,128,4,128]{3,2,0,1:T(4,128)(2,1)}, u32[]{:S(2)}, u32[]{:S(2)}) %all-to-all-start.3) | async-done | bytes 8388640 | tf_op jit(solution)/shard_map/all_to_all | solution.py:83
  634.4 5.8 all-to-all-start.2
  640.4 16.3 %copy.49 = bf16[64,128,4,128]{3,1,2,0:T(8,128)(2,1)} copy(bf16[64,128,4,128]{3,2,0,1:T(4,128)(2,1)} %all-to-all-done.3) | data formatting | bytes 16777216 | tf_op jit(solution)/shard_map/all_to_all | solution.py:83
  656.7 9.3 copy.50
  665.9 13.7 %copy.52 = bf16[256,32,4,128]{0,3,2,1:T(8,128)(2,1)} copy(bf16[256,32,4,128]{3,1,2,0:T(8,128)(2,1)} %bitcast.82) | data formatting | bytes 16777216
  679.7 53.9 %all-to-all-done.2 = bf16[64,128,4,128]{3,0,2,1:T(8,128)(2,1)} async-done(((bf16[64,128,4,128]{3,0,2,1:T(8,128)(2,1)}), bf16[64,128,4,128]{3,0,2,1:T(8,128)(2,1)}, u32[]{:S(2)}, u32[]{:S(2)}) %all-to-all-start.2) | async-done | bytes 8388640 | tf_op jit(solution)/shard_map/all_to_all | solution.py:82
  733.6 12.0 %copy.44 = bf16[4,64,32,4,128]{4,2,3,1,0:T(8,128)(2,1)} copy(bf16[4,64,32,4,128]{4,1,3,2,0:T(8,128)(2,1)} %bitcast.15) | data formatting | bytes 16777216 | tf_op jit(solution)/shard_map/all_to_all | solution.py:82
  745.7 13.8 %copy.51 = bf16[256,32,4,128]{0,3,2,1:T(8,128)(2,1)} copy(bf16[256,32,4,128]{3,1,2,0:T(8,128)(2,1)} %bitcast.83) | data formatting | bytes 16777216
  759.4 382.9 %while.11 = (s32[]{:T(128)}, f32[32,1,4,512]{3,2,1,0:T(4,128)S(1)}, s32[32]{0:T(128)S(1)}, bf16[256,32,4,128]{0,3,2,1:T(8,128)(2,1)}, bf16[256,32,4,128]{0,3,2,1...) while((s32[]{:T(128)}, f32[32,1,4,512]{3,2,1,0:T(4,128)S(1)}, ...), condition=%wide.region_2.3_spmd.clone, body=%wide.region_0.0_spmd.clone.sunk | while | flops 1616637952 | bytes 8942751 | solution.py:57
  766.0 4.0 convolution_bitcast_fusion.5
  777.9 4.0 convolution_bitcast_fusion.5
  789.9 4.0 convolution_bitcast_fusion.5
  813.8 4.0 convolution_bitcast_fusion.5
  825.7 4.0 convolution_bitcast_fusion.5
  837.7 4.0 convolution_bitcast_fusion.5
  849.7 4.0 convolution_bitcast_fusion.5
  861.6 4.0 convolution_bitcast_fusion.5
  873.6 4.0 convolution_bitcast_fusion.5
  897.5 4.0 convolution_bitcast_fusion.5
  909.4 4.0 convolution_bitcast_fusion.5
  1145.6 8.4 all_to_all.90
  (277 shorter events, 288.9 us)
Async XLA Ops:
  1.8 16.2 %all-to-all-start = ((s32[4,128,128]{2,0,1:T(4,128)}), s32[4,128,128]{2,0,1:T(4,128)S(1)}, u32[]{:S(2)}, u32[]{:S(2)}) async-start(s32[4,128,128]{2,0,1:T(4,128)} %copy.36), calls=%async_computation | async-start | bytes 524288 | tf_op jit(solution)/shard_map/all_to_all | solution.py:70
  270.8 6.2 copy-start
  270.8 263.6 %all-to-all-start.1 = ((bf16[64,4,128,128]{3,0,1,2:T(8,128)(2,1)}), bf16[64,4,128,128]{3,0,1,2:T(8,128)(2,1)}, u32[]{:S(2)}, u32[]{:S(2)}) async-start(bf16[64,4,128,128]{3,0,1,2:T(8,128)(2,1)} %select_bitcast_fusion.1), calls=%async_computation.1 | async-start | bytes 16777216 | tf_op jit(solution)/shard_map/all_to_all | solution.py:79
  506.4 19.2 %copy-start.1 = (s32[4,128]{1,0:T(4,128)S(1)}, s32[4,128]{1,0:T(4,128)}, u32[]{:S(2)}) copy-start(s32[4,128]{1,0:T(4,128)} %param.7) | copy-start | bytes 6148
  534.4 100.0 %all-to-all-start.3 = ((bf16[64,128,4,128]{3,2,0,1:T(4,128)(2,1)}), bf16[64,128,4,128]{3,2,0,1:T(4,128)(2,1)}, u32[]{:S(2)}, u32[]{:S(2)}) async-start(bf16[64,128,4,128]{3,2,0,1:T(4,128)(2,1)} %select_bitcast_fusion), calls=%async_computation.3 | async-start | bytes 16777216 | tf_op jit(solution)/shard_map/all_to_all | solution.py:83
  634.4 99.2 %all-to-all-start.2 = ((bf16[64,128,4,128]{3,0,2,1:T(8,128)(2,1)}), bf16[64,128,4,128]{3,0,2,1:T(8,128)(2,1)}, u32[]{:S(2)}, u32[]{:S(2)}) async-start(bf16[64,128,4,128]{3,0,2,1:T(8,128)(2,1)} %bitcast.80), calls=%async_computation.2 | async-start | bytes 16777216 | tf_op jit(solution)/shard_map/all_to_all | solution.py:82
where the time goes:
time: 1160 us
  local copies, waits for them, and re-layouts  597 us (51%)
  matrix products  259 us (22%)
  waiting for transfers between devices  143 us (12%)
  loops' own time  61.9 us (5%)
  other arithmetic  60.3 us (5%)
  starting transfers between devices  26.1 us (2%)
    gather x2, local copies, waits for them, and re-layouts, body(): own_traces = jnp.take(flat_signals, own_index, axis=1)  248 us
    gather x2, local copies, waits for them, and re-layouts, body(): remote_side = jnp.take(flat_signals, sender_index, axis=1)  245 us
    dot_general x32, matrix products, one_block(): jnp.einsum('tsrj,tk->srjk', part_a, forward, precision=lax.Precision.HIGH...  128 us
    dot_general x32, matrix products, one_block(): jnp.einsum('tsrj,tk->srjk', part_b, forward, precision=lax.Precision.HIGH...  128 us
    all_to_all x1, waiting for transfers between devices, body(): lax.all_to_all(local_side, 'tm', split_axis=1, concat_axis=0, tiled=True)  84.8 us
    another operation x1, loops' own time, predict(): spectra = lax.map(one_block, jnp.arange(blocks, dtype=jnp.int32))  61.9 us
    all_to_all x1, waiting for transfers between devices, body(): lax.all_to_all(arrived, 'tm', split_axis=1, concat_axis=0, tiled=True)  53.9 us
    unnamed x10, local copies, waits for them, and re-layouts  32.9 us
  transfers between devices with their start and end apart: 4, of which 3 were waited for; matrix products, arithmetic and copies ran while one was open for 27% of the time, Pallas kernels for 0%

commit v1 on v0

--- a/solution.py
+++ b/solution.py
@@ -79,7 +79,12 @@
     arrived = lax.all_to_all(remote_side, "shot", split_axis=2, concat_axis=1, tiled=True)
     merged = convolve(
         (
-            lax.all_to_all(arrived, "tm", split_axis=1, concat_axis=0, tiled=True),
+            jnp.concatenate(
+                lax.all_to_all(
+                    jnp.stack(jnp.split(arrived, lax.axis_size("tm"), axis=1)), "tm", 0, 0
+                ),
+                axis=0,
+            ),
             lax.all_to_all(local_side, "tm", split_axis=1, concat_axis=0, tiled=True),
         )
     )

time: 1160 us -> 1150 us (level)
  local copies, waits for them, and re-layouts: 597 us -> 582 us
    all_to_all x1 -> x0, local copies, waits for them, and re-layouts: 12 us -> none  [body(): lax.all_to_all(arrived, 'tm', split_axis=1, concat_axis=0, tiled=True)]
where the time goes in v1:
time: 1150 us; the launch traced here: 1140 us
  local copies, waits for them, and re-layouts  582 us (51%)
  matrix products  259 us (23%)
  waiting for transfers between devices  140 us (12%)
  other arithmetic  64.1 us (6%)
  loops' own time  61.6 us (5%)
  starting transfers between devices  26.2 us (2%)
    gather x2, local copies, waits for them, and re-layouts, body(): own_traces = jnp.take(flat_signals, own_index, axis=1)  246 us
    gather x2, local copies, waits for them, and re-layouts, body(): remote_side = jnp.take(flat_signals, sender_index, axis=1)  243 us
    dot_general x32, matrix products, one_block(): jnp.einsum('tsrj,tk->srjk', part_a, forward, precision=lax.Precision.HIGH...  128 us
    dot_general x32, matrix products, one_block(): jnp.einsum('tsrj,tk->srjk', part_b, forward, precision=lax.Precision.HIGH...  128 us
    all_to_all x1, waiting for transfers between devices, body(): lax.all_to_all(local_side, 'tm', split_axis=1, concat_axis=0, tiled=True)  81.2 us
    another operation x1, loops' own time, predict(): spectra = lax.map(one_block, jnp.arange(blocks, dtype=jnp.int32))  61.6 us
    all_to_all x1, waiting for transfers between devices, body(): lax.all_to_all(jnp.stack(jnp.split(arrived, lax.axis_size('tm'), axis=1))...  54 us
    unnamed x10, local copies, waits for them, and re-layouts  32.8 us
  transfers between devices with their start and end apart: 4, of which 3 were waited for; matrix products, arithmetic and copies ran while one was open for 27% of the time, Pallas kernels for 0%

profile of v1, /device:TPU:8, one launch (start us, length us, event | category | flops | bytes accessed | tf_op | source)
XLA Modules:
  0.0 1141.3 jit_solution(11945318716810012306)
XLA Ops:
  1.8 8.5 all-to-all-start
  13.3 4.8 all-to-all-done
  18.3 227.3 %gather_fusion = bf16[65536,64]{1,0:T(8,128)(2,1)} fusion(bf16[64,8192]{0,1:T(8,128)(2,1)S(1)} %bitcast.81, s32[65536]{0:T(1024)S(1)} %broadcast_clamp_fusion.1), kind=kCustom, calls=%fused_computation | custom fusion | bytes 17039360 | tf_op jit(solution)/shard_map/jit(_take)/gather | solution.py:78
  245.6 15.8 %copy.40 = bf16[4,128,128,64]{2,3,0,1:T(8,128)(2,1)} copy(bf16[4,128,128,64]{3,2,1,0:T(8,128)(2,1)} %bitcast.84) | data formatting | bytes 16777216 | tf_op jit(solution)/shard_map/jit(_take)/gather | solution.py:78
  261.6 7.6 select_bitcast_fusion.1
  269.1 6.1 all-to-all-start.1
  275.7 227.3 %gather_fusion.1 = bf16[65536,64]{1,0:T(8,128)(2,1)} fusion(bf16[64,8192]{0,1:T(8,128)(2,1)S(1)} %bitcast.82, s32[65536]{0:T(1024)S(1)} %broadcast_clamp_fusion), kind=kCustom, calls=%fused_computation.1 | custom fusion | bytes 17039360 | tf_op jit(solution)/shard_map/jit(_take)/gather | solution.py:76
  503.0 19.1 %copy.45 = bf16[128,4,128,64]{2,1,3,0:T(4,128)(2,1)} copy(bf16[128,4,128,64]{3,2,1,0:T(8,128)(2,1)} %bitcast.83) | data formatting | bytes 16777216 | tf_op jit(solution)/shard_map/jit(_take)/gather | solution.py:76
  522.5 8.5 select_bitcast_fusion
  531.0 5.7 all-to-all-start.3
  536.7 6.8 copy.41
  549.9 81.2 %all-to-all-done.3 = bf16[64,128,4,128]{3,2,0,1:T(4,128)(2,1)} async-done(((bf16[64,128,4,128]{3,2,0,1:T(4,128)(2,1)}), bf16[64,128,4,128]{3,2,0,1:T(4,128)(2,1)}, u32[]{:S(2)}, u32[]{:S(2)}) %all-to-all-start.3) | async-done | bytes 8388640 | tf_op jit(solution)/shard_map/all_to_all | solution.py:88
  631.1 5.8 all-to-all-start.2
  637.0 16.3 %copy.46 = bf16[64,128,4,128]{3,1,2,0:T(8,128)(2,1)} copy(bf16[64,128,4,128]{3,2,0,1:T(4,128)(2,1)} %all-to-all-done.3) | data formatting | bytes 16777216 | tf_op jit(solution)/shard_map/all_to_all | solution.py:88
  653.3 9.3 copy.47
  662.6 13.7 %copy.49 = bf16[256,32,4,128]{0,3,2,1:T(8,128)(2,1)} copy(bf16[256,32,4,128]{3,1,2,0:T(8,128)(2,1)} %bitcast.87) | data formatting | bytes 16777216
  676.3 54.0 %all-to-all-done.2 = bf16[4,64,32,4,128]{4,2,3,1,0:T(8,128)(2,1)} async-done(((bf16[4,64,32,4,128]{4,2,3,1,0:T(8,128)(2,1)}), bf16[4,64,32,4,128]{4,2,3,1,0:T(8,128)(2,1)}, u32[]{:S(2)}, u32[]{:S(2)}) %all-to-all-start.2) | async-done | bytes 8388640 | tf_op jit(solution)/shard_map/all_to_all | solution.py:83
  730.3 13.7 %copy.48 = bf16[256,32,4,128]{0,3,2,1:T(8,128)(2,1)} copy(bf16[256,32,4,128]{3,1,2,0:T(8,128)(2,1)} %bitcast.17) | data formatting | bytes 16777216
  744.0 382.9 %while.11 = (s32[]{:T(128)}, f32[32,1,4,512]{3,2,1,0:T(4,128)S(1)}, s32[32]{0:T(128)S(1)}, bf16[256,32,4,128]{0,3,2,1:T(8,128)(2,1)}, bf16[256,32,4,128]{0,3,2,1...) while((s32[]{:T(128)}, f32[32,1,4,512]{3,2,1,0:T(4,128)S(1)}, ...), condition=%wide.region_2.3_spmd.clone, body=%wide.region_0.0_spmd.clone.sunk | while | flops 1616637952 | bytes 8942751 | solution.py:57
  786.5 4.0 convolution_bitcast_fusion.5
  798.4 4.0 convolution_bitcast_fusion.5
  810.4 4.0 convolution_bitcast_fusion.5
  822.4 4.0 convolution_bitcast_fusion.5
  846.3 4.0 convolution_bitcast_fusion.5
  858.2 4.0 convolution_bitcast_fusion.5
  870.2 4.0 convolution_bitcast_fusion.5
  882.2 4.0 convolution_bitcast_fusion.5
  906.1 4.0 convolution_bitcast_fusion.5
  918.1 4.0 convolution_bitcast_fusion.5
  930.0 4.0 convolution_bitcast_fusion.5
  954.0 4.0 convolution_bitcast_fusion.5
  1130.2 8.4 all_to_all.77
  (278 shorter events, 291.5 us)
Async XLA Ops:
  1.8 16.2 %all-to-all-start = ((s32[4,128,128]{2,0,1:T(4,128)}), s32[4,128,128]{2,0,1:T(4,128)S(1)}, u32[]{:S(2)}, u32[]{:S(2)}) async-start(s32[4,128,128]{2,0,1:T(4,128)} %copy.36), calls=%async_computation | async-start | bytes 524288 | tf_op jit(solution)/shard_map/all_to_all | solution.py:70
  269.1 6.2 copy-start
  269.1 261.9 %all-to-all-start.1 = ((bf16[64,4,128,128]{3,0,1,2:T(8,128)(2,1)}), bf16[64,4,128,128]{3,0,1,2:T(8,128)(2,1)}, u32[]{:S(2)}, u32[]{:S(2)}) async-start(bf16[64,4,128,128]{3,0,1,2:T(8,128)(2,1)} %select_bitcast_fusion.1), calls=%async_computation.1 | async-start | bytes 16777216 | tf_op jit(solution)/shard_map/all_to_all | solution.py:79
  503.0 19.2 %copy-start.1 = (s32[4,128]{1,0:T(4,128)S(1)}, s32[4,128]{1,0:T(4,128)}, u32[]{:S(2)}) copy-start(s32[4,128]{1,0:T(4,128)} %param.7) | copy-start | bytes 6148
  531.0 100.1 %all-to-all-start.3 = ((bf16[64,128,4,128]{3,2,0,1:T(4,128)(2,1)}), bf16[64,128,4,128]{3,2,0,1:T(4,128)(2,1)}, u32[]{:S(2)}, u32[]{:S(2)}) async-start(bf16[64,128,4,128]{3,2,0,1:T(4,128)(2,1)} %select_bitcast_fusion), calls=%async_computation.3 | async-start | bytes 16777216 | tf_op jit(solution)/shard_map/all_to_all | solution.py:88
  631.1 99.2 %all-to-all-start.2 = ((bf16[4,64,32,4,128]{4,2,3,1,0:T(8,128)(2,1)}), bf16[4,64,32,4,128]{4,2,3,1,0:T(8,128)(2,1)}, u32[]{:S(2)}, u32[]{:S(2)}) async-start(bf16[4,64,32,4,128]{4,2,3,1,0:T(8,128)(2,1)} %pad_maximum_fusion), calls=%async_computation.2 | async-start | bytes 16777216 | tf_op jit(solution)/shard_map/all_to_all | solution.py:83
